TPU v7x, 256 devices: a whole 4x4x8 slice. The times are simulated.
256 devices in a mesh: seq: 64 (over z, y, core), ch: 4 (over x).
Axes of the slice: x: 4, y: 4, z: 8, core: 2. Of those that a mesh axis runs over, the one named last changes fastest.
Arguments:
- query_proj: bfloat16 [8192, 2048], P('seq', 'ch'), may hold values from -6 to 6
- key_proj: bfloat16 [8192, 2048], P('seq', 'ch'), may hold values from -6 to 6
- value_proj: bfloat16 [8192, 2048], P('seq', 'ch'), may hold values from -6 to 6
- short_filter: float32 [3, 3, 2048], P(None, None, 'ch'), may hold values from -3.5 to 3.5
- long_filter: float32 [8192, 2048], P('seq', 'ch'), may hold values from -0.0625 to 0.0625
- skip_gain: float32 [2048], P('ch'), may hold values from 0.5 to 1.5
- out_weight: bfloat16 [2048, 4096], P('ch'), may hold values from -0.125 to 0.125
- cotangent: bfloat16 [8192, 4096], P('seq', 'ch'), may hold values from -16 to 16
Outputs:
- layer_out: bfloat16 [8192, 4096], P('seq', 'ch')
- grad_query: float32 [8192, 2048], P('seq', 'ch')
- grad_key: float32 [8192, 2048], P('seq', 'ch')
- grad_value: float32 [8192, 2048], P('seq', 'ch')
- grad_short: float32 [3, 3, 2048], P(None, None, 'ch')
- grad_filter: float32 [8192, 2048], P('seq', 'ch')
- grad_skip: float32 [2048], P('ch')
- grad_w_out_t: float32 [4096, 2048], P('seq', 'ch')
All inputs are finite; a program needn't handle non-finite values.
Results may differ from a plain program's by a relative error of at most 0.011.
Values may be sent and summed in bfloat16 or wider, within the bound.
A program may use at most 128 MiB of HBM per device.

v0:
```python
import math
import jax
import jax.numpy as jnp
from jax import lax
from jax.sharding import PartitionSpec as P

exact_mode = lax.Precision.HIGHEST


def from_behind(shard, axis, by):
    size = lax.axis_size(axis)
    pairs = [(i, i + by) for i in range(size) if 0 <= i + by < size]
    return lax.ppermute(shard, axis, pairs)


def as_sent(shard):

    def short(part):
        return part.astype(jnp.bfloat16) if part.dtype == jnp.float32 else part

    return jax.tree.map(short, shard)


def split_lanes(merged, lanes):
    return tuple(
        (merged[..., start : start + lanes] for start in range(0, merged.shape[-1], lanes))
    )


def tables(rows_out, cols_in, period):
    row_index = lax.broadcasted_iota(jnp.int32, (rows_out, cols_in), 0)
    col_index = lax.broadcasted_iota(jnp.int32, (rows_out, cols_in), 1)
    phase_angle = (row_index * col_index % period).astype(jnp.float32) * (2.0 * math.pi / period)
    return (jnp.cos(phase_angle), jnp.sin(phase_angle))


def along_rows(factor, values):
    return jnp.tensordot(factor, values, axes=1, precision=exact_mode)


def rows_spectrum(signal, basis_pair):
    return (along_rows(basis_pair[0], signal), -along_rows(basis_pair[1], signal))


def rows_inverse(complex_pair, basis_pair):
    total = along_rows(basis_pair[0], complex_pair[0]) - along_rows(basis_pair[1], complex_pair[1])
    return total / basis_pair[0].shape[1]


def block_forward(complex_pair, basis_pair):
    cosine_part, sine_part = basis_pair
    real_part = along_rows(cosine_part, complex_pair[0]) + along_rows(sine_part, complex_pair[1])
    imag_part = along_rows(cosine_part, complex_pair[1]) - along_rows(sine_part, complex_pair[0])
    return (real_part, imag_part)


def block_inverse(complex_pair, basis_pair):
    cosine_part, sine_part = basis_pair
    norming = 1.0 / cosine_part.shape[1]
    real_part = along_rows(cosine_part, complex_pair[0]) - along_rows(sine_part, complex_pair[1])
    imag_part = along_rows(cosine_part, complex_pair[1]) + along_rows(sine_part, complex_pair[0])
    return (real_part * norming, imag_part * norming)


def complex_product(first_pair, second_pair):
    return (
        first_pair[0] * second_pair[0] - first_pair[1] * second_pair[1],
        first_pair[0] * second_pair[1] + first_pair[1] * second_pair[0],
    )


def conj_product(first_pair, second_pair):
    return (
        first_pair[0] * second_pair[0] + first_pair[1] * second_pair[1],
        first_pair[0] * second_pair[1] - first_pair[1] * second_pair[0],
    )


def on_device(
    query_proj, key_proj, value_proj, short_filter, long_filter, skip_gain, out_weight, cotangent
):
    block_rows = query_proj.shape[0]
    tap_count = short_filter.shape[1]
    block_count = lax.axis_size("seq")
    streams = jnp.stack([query_proj, key_proj, value_proj])
    earlier = from_behind(streams[:, block_rows - (tap_count - 1) :], "seq", 1)
    extended = jnp.concatenate([earlier, streams], axis=1).astype(jnp.float32)
    shifted = [
        extended[:, tap_count - 1 - offset : tap_count - 1 - offset + block_rows]
        for offset in range(tap_count)
    ]
    filtered = sum(
        (short_filter[:, offset][:, None, :] * shifted[offset] for offset in range(tap_count))
    )
    query_short, key_short, value_short = (filtered[0], filtered[1], filtered[2])
    product = key_short * value_short
    forward_basis = tables(2 * block_rows, block_rows, 2 * block_rows)
    full_basis = tables(2 * block_rows, 2 * block_rows, 2 * block_rows)
    half_basis = tables(block_rows, 2 * block_rows, 2 * block_rows)
    block_basis = tables(2 * block_count, block_count, 2 * block_count)
    return_basis = tables(block_count, 2 * block_count, 2 * block_count)
    input_pair = rows_spectrum(product, forward_basis)
    filter_pair = rows_spectrum(long_filter, forward_basis)
    lanes = product.shape[1]
    moved_data = split_lanes(
        lax.all_to_all(
            jnp.concatenate([input_pair[0], input_pair[1], filter_pair[0], filter_pair[1]], axis=1)[
                None
            ],
            "seq",
            split_axis=1,
            concat_axis=0,
            tiled=True,
        ),
        lanes,
    )
    input_spectrum = block_forward((moved_data[0], moved_data[1]), block_basis)
    filter_spectrum = block_forward((moved_data[2], moved_data[3]), block_basis)
    inverse_pair = block_inverse(complex_product(filter_spectrum, input_spectrum), return_basis)
    returned = split_lanes(
        lax.all_to_all(
            jnp.concatenate(inverse_pair, axis=-1), "seq", split_axis=0, concat_axis=1, tiled=True
        ),
        lanes,
    )
    folded = rows_inverse((returned[0][0], returned[1][0]), full_basis)
    carried = from_behind(folded[block_rows:], "seq", 1)
    convolved = folded[:block_rows] + carried
    mixed_seq = convolved + skip_gain * product
    gated_values = (query_short * mixed_seq).astype(jnp.bfloat16)
    partial_value = jnp.dot(gated_values, out_weight, preferred_element_type=jnp.float32)
    layer_out = lax.psum_scatter(partial_value, "ch", scatter_dimension=1, tiled=True).astype(
        jnp.bfloat16
    )
    full_cotangent = lax.all_gather(cotangent, "ch", axis=1, tiled=True)
    grad_gated = lax.dot_general(
        full_cotangent, out_weight, (((1,), (1,)), ((), ())), preferred_element_type=jnp.float32
    )
    weight_terms = lax.dot_general(
        full_cotangent, gated_values, (((0,), (0,)), ((), ())), preferred_element_type=jnp.float32
    )
    grad_mixed = grad_gated * query_short
    grad_query_short = grad_gated * mixed_seq
    following = from_behind(grad_mixed.astype(jnp.bfloat16), "seq", -1).astype(grad_mixed.dtype)
    spread = jnp.concatenate([grad_mixed, following], axis=0)
    grad_pair = rows_spectrum(spread, full_basis)
    moved_grad = split_lanes(
        lax.all_to_all(
            jnp.concatenate(grad_pair, axis=1)[None].astype(jnp.bfloat16),
            "seq",
            split_axis=1,
            concat_axis=0,
            tiled=True,
        ).astype(jnp.float32),
        lanes,
    )
    grad_spectrum = block_forward(moved_grad, block_basis)
    input_back = block_inverse(conj_product(filter_spectrum, grad_spectrum), return_basis)
    filter_back = block_inverse(conj_product(input_spectrum, grad_spectrum), return_basis)
    returned_grad = split_lanes(
        lax.all_to_all(
            as_sent(jnp.concatenate(input_back + filter_back, axis=-1)),
            "seq",
            split_axis=0,
            concat_axis=1,
            tiled=True,
        ),
        lanes,
    )
    conv_grad = rows_inverse((returned_grad[0][0], returned_grad[1][0]), half_basis)
    grad_filter = rows_inverse((returned_grad[2][0], returned_grad[3][0]), half_basis)
    grad_product = conv_grad + skip_gain * grad_mixed
    grad_streams = jnp.stack(
        [grad_query_short, grad_product * value_short, grad_product * key_short]
    )
    later_rows = from_behind(grad_streams[:, : tap_count - 1], "seq", -1)
    padded_grad = jnp.concatenate([grad_streams, later_rows], axis=1)
    grad_inputs = sum(
        (
            short_filter[:, offset][:, None, :] * padded_grad[:, offset : offset + block_rows]
            for offset in range(tap_count)
        )
    )
    short_terms = jnp.stack(
        [jnp.sum(grad_streams * shifted[offset], axis=1) for offset in range(tap_count)], axis=1
    )
    skip_terms = jnp.sum(grad_mixed * product, axis=0)
    channel_count = skip_terms.shape[0]
    sum_rows = short_terms.shape[0] * short_terms.shape[1] + 1
    padded_rows = -(-sum_rows // 8) * 8
    small_terms = jnp.concatenate(
        [
            short_terms.reshape(sum_rows - 1, channel_count),
            skip_terms[None],
            jnp.zeros((padded_rows - sum_rows, channel_count), jnp.float32),
        ]
    )
    weight_blocks = weight_terms.reshape(block_count, -1, channel_count)
    block_height = weight_blocks.shape[1]
    combined = jnp.concatenate(
        [weight_blocks, jnp.broadcast_to(small_terms, (block_count, padded_rows, channel_count))],
        axis=1,
    )
    reduced = lax.psum_scatter(
        combined.reshape(-1, channel_count), "seq", scatter_dimension=0, tiled=True
    )
    grad_w_out_t = reduced[:block_height]
    grad_short = reduced[block_height : block_height + sum_rows - 1].reshape(short_terms.shape)
    grad_skip = reduced[block_height + sum_rows - 1]
    return (
        layer_out,
        grad_inputs[0],
        grad_inputs[1],
        grad_inputs[2],
        grad_short,
        grad_filter,
        grad_skip,
        grad_w_out_t,
    )


def solution(mesh):
    in_specs = (
        P("seq", "ch"),
        P("seq", "ch"),
        P("seq", "ch"),
        P(None, None, "ch"),
        P("seq", "ch"),
        P("ch"),
        P("ch", None),
        P("seq", "ch"),
    )
    out_specs = (
        P("seq", "ch"),
        P("seq", "ch"),
        P("seq", "ch"),
        P("seq", "ch"),
        P(None, None, "ch"),
        P("seq", "ch"),
        P("ch"),
        P("seq", "ch"),
    )
    return jax.shard_map(
        on_device, mesh=mesh, in_specs=in_specs, out_specs=out_specs, check_vma=False
    )
```

profile of v0, /device:TPU:2, one launch (start us, length us, event | category | flops | bytes accessed | tf_op | source)
XLA Modules:
  0.0 450.7 jit_solution(9208655784076676578)
XLA Ops:
  12.7 25.7 %all-gather.2.cloned.1.call-done = bf16[128,4096]{1,0:T(8,128)(2,1)} async-done(((bf16[128,1024]{1,0:T(8,128)(2,1)}), bf16[128,4096]{1,0:T(8,128)(2,1)}) %all-gather.2.cloned.1.call-update) | async-done | bytes 1048592 | tf_op jit(solution)/shard_map/all_gather | solution.py:135
  38.4 4.8 %multiply_reduce_fusion.3 = (f32[512]{0:T(512)S(1)}, f32[128,512]{1,0:T(8,128)S(1)}, f32[128,512]{1,0:T(8,128)S(1)}, f32[128,512]{1,0:T(8,128)}) fusion(f32[3,128,512]{2,1,0:T(8,128)S(1)} %multiply_add_fusion.3, bf16[128,4096]{1,0:T(8,128)(2,1)} %all-gather.2.cloned.1.call-done, bf16[512,4096]{1,0:T(8,128)(2,1)} %param.14), kind=kOutput, calls=%fused_computation.95 | convolution fusion | flops 537132544 | bytes 6817792 | tf_op jit(solution)/shard_map/dot_general | solution.py:136
  51.1 3.7 reduce.3
  56.0 13.8 %all-to-all-start.2 = ((bf16[64,2,2048]{2,1,0:T(2,128)(2,1)}), bf16[64,2,2048]{2,1,0:T(2,128)(2,1)S(1)}, u32[]{:S(2)}, u32[]{:S(2)}) async-start(bf16[64,2,2048]{2,1,0:T(2,128)(2,1)} %reshape.83), calls=%async_computation.3 | async-start | bytes 1048576 | tf_op jit(solution)/shard_map/all_to_all | solution.py:148
  74.2 3.5 copy.39
  77.7 9.7 %all-to-all-done.2 = bf16[64,2,2048]{2,1,0:T(2,128)(2,1)S(1)} async-done(((bf16[64,2,2048]{2,1,0:T(2,128)(2,1)}), bf16[64,2,2048]{2,1,0:T(2,128)(2,1)S(1)}, u32[]{:S(2)}, u32[]{:S(2)}) %all-to-all-start.2) | async-done | bytes 524320 | tf_op jit(solution)/shard_map/all_to_all | solution.py:148
  88.2 5.8 %all-to-all-start = ((f32[1,256,2048]{2,0,1:T(1,128)}), f32[1,256,2048]{2,0,1:T(1,128)S(1)}, u32[]{:S(2)}, u32[]{:S(2)}) async-start(f32[1,256,2048]{2,0,1:T(1,128)} %copy.39), calls=%async_computation | async-start | bytes 4194304 | tf_op jit(solution)/shard_map/all_to_all | solution.py:106
  94.0 4.8 %reshape.84 = bf16[256,1,1024]{2,1,0:T(2,128)(2,1)} reshape(bf16[64,2,2048]{2,1,0:T(2,128)(2,1)} %copy-done.13) | data formatting | bytes 1048576
  98.9 5.1 %bitcast_reduce_fusion = bf16[256,1024]{1,0:T(8,128)(2,1)} fusion(bf16[256,1,1024]{2,1,0:T(2,128)(2,1)} %reshape.84), kind=kLoop, calls=%fused_computation.345 | loop fusion | bytes 1048576 | tf_op jit(solution)/shard_map/all_to_all | solution.py:148
  104.0 2.0 all_to_all.41
  112.2 33.2 %all-to-all-done = f32[1,256,2048]{2,0,1:T(1,128)S(1)} async-done(((f32[1,256,2048]{2,0,1:T(1,128)}), f32[1,256,2048]{2,0,1:T(1,128)S(1)}, u32[]{:S(2)}, u32[]{:S(2)}) %all-to-all-start) | async-done | bytes 2097184 | tf_op jit(solution)/shard_map/all_to_all | solution.py:106
  145.4 6.8 %reduce = f32[256,2048]{1,0:T(8,128)} reduce(f32[1,256,2048]{2,0,1:T(1,128)S(1)} %all-to-all-done, f32[]{:T(128)} %constant.71), dimensions={0}, to_apply=%all_to_all.16.reduce_sub_computation | reduce | bytes 4194308 | tf_op jit(solution)/shard_map/all_to_all | solution.py:106
  152.2 2.0 all_to_all.17
  163.0 2.8 multiply_add_fusion.1
  172.6 5.6 %all-to-all-start.1 = ((f32[64,4,1024]{2,1,0:T(4,128)}), f32[64,4,1024]{2,1,0:T(4,128)}, u32[]{:S(2)}, u32[]{:S(2)}) async-start(f32[64,4,1024]{2,1,0:T(4,128)} %copy.44), calls=%async_computation.1 | async-start | bytes 2097152 | tf_op jit(solution)/shard_map/all_to_all | solution.py:121
  186.2 20.8 %all-to-all-done.1 = f32[64,4,1024]{2,1,0:T(4,128)} async-done(((f32[64,4,1024]{2,1,0:T(4,128)}), f32[64,4,1024]{2,1,0:T(4,128)}, u32[]{:S(2)}, u32[]{:S(2)}) %all-to-all-start.1) | async-done | bytes 1048608 | tf_op jit(solution)/shard_map/all_to_all | solution.py:121
  206.9 5.8 %all-to-all-start.3 = ((bf16[64,4,2048]{2,1,0:T(4,128)(2,1)}), bf16[64,4,2048]{2,1,0:T(4,128)(2,1)S(1)}, u32[]{:S(2)}, u32[]{:S(2)}) async-start(bf16[64,4,2048]{2,1,0:T(4,128)(2,1)} %copy.48), calls=%async_computation.4 | async-start | bytes 2097152 | tf_op jit(solution)/shard_map/all_to_all | solution.py:161
  218.5 2.9 collective-permute-start.1
  221.4 20.3 %all-to-all-done.3 = bf16[64,4,2048]{2,1,0:T(4,128)(2,1)S(1)} async-done(((bf16[64,4,2048]{2,1,0:T(4,128)(2,1)}), bf16[64,4,2048]{2,1,0:T(4,128)(2,1)S(1)}, u32[]{:S(2)}, u32[]{:S(2)}) %all-to-all-start.3) | async-done | bytes 1048608 | tf_op jit(solution)/shard_map/all_to_all | solution.py:161
  247.7 2.1 fusion.303
  251.4 4.5 %convolution_bitcast_fusion = f32[4096,512]{0,1:T(8,128)} fusion(bf16[128,512]{1,0:T(8,128)(2,1)S(1)} %get-tuple-element.36, bf16[128,4096]{1,0:T(8,128)(2,1)S(1)} %copy-done.10), kind=kOutput, calls=%fused_computation.1 | convolution fusion | flops 536870912 | bytes 9568256 | tf_op jit(solution)/shard_map/dot_general | solution.py:139
  255.9 9.1 %copy.49 = f32[4096,512]{1,0:T(8,128)} copy(f32[4096,512]{0,1:T(8,128)} %convolution_bitcast_fusion) | data formatting | bytes 16777216 | tf_op jit(solution)/shard_map/dot_general | solution.py:139
  266.9 9.7 %pad_maximum_fusion = f32[64,80,512]{2,1,0:T(8,128)} fusion(f32[64,16,512]{2,1,0:T(8,128)S(1)} %broadcast_in_dim.18, f32[64,64,512]{2,1,0:T(8,128)} %bitcast.158), kind=kLoop, calls=%fused_computation | loop fusion | flops 2621440 | bytes 20971520 | tf_op jit(solution)/shard_map/concatenate | solution.py:200
  282.8 156.7 %reduce-scatter.5.cloned.1.call-done = f32[80,512]{1,0:T(8,128)} async-done(((f32[5120,512]{1,0:T(8,128)}), f32[80,512]{1,0:T(8,128)}) %reduce-scatter.5.cloned.1.call-update) | async-done | bytes 163856 | tf_op jit(solution)/shard_map/reduce_scatter | solution.py:204
  (132 shorter events, 74.5 us)
Async XLA Ops:
  7.2 62.6 %copy-start = (f32[128,512]{1,0:T(8,128)S(1)}, f32[128,512]{1,0:T(8,128)}, u32[]{:S(2)}) copy-start(f32[128,512]{1,0:T(8,128)} %param.12) | copy-start | bytes 786436
  7.2 31.2 %all-gather.2.cloned.1.call-start = ((), (), s32[]{:S(2)}) async-start(), calls=%async_computation.7 | async-start | bytes 1310720 | tf_op jit(solution)/shard_map/all_gather | solution.py:135
  8.7 2.6 collective-permute-start
  12.7 30.4 %copy-start.6 = (f32[3,128,512]{2,1,0:T(8,128)}, f32[3,128,512]{2,1,0:T(8,128)S(1)}, u32[]{:S(2)}) copy-start(f32[3,128,512]{2,1,0:T(8,128)S(1)} %multiply_add_fusion.3) | copy-start | bytes 2359300
  43.2 6.6 %copy-start.16 = (f32[128,512]{1,0:T(8,128)}, f32[128,512]{1,0:T(8,128)S(1)}, u32[]{:S(2)}) copy-start(f32[128,512]{1,0:T(8,128)S(1)} %get-tuple-element.12) | copy-start | bytes 786436
  43.2 3.2 collective-permute-start.2
  56.0 31.5 %all-to-all-start.2 = ((bf16[64,2,2048]{2,1,0:T(2,128)(2,1)}), bf16[64,2,2048]{2,1,0:T(2,128)(2,1)S(1)}, u32[]{:S(2)}, u32[]{:S(2)}) async-start(bf16[64,2,2048]{2,1,0:T(2,128)(2,1)} %reshape.83), calls=%async_computation.3 | async-start | bytes 1048576 | tf_op jit(solution)/shard_map/all_to_all | solution.py:148
  88.2 57.2 %all-to-all-start = ((f32[1,256,2048]{2,0,1:T(1,128)}), f32[1,256,2048]{2,0,1:T(1,128)S(1)}, u32[]{:S(2)}, u32[]{:S(2)}) async-start(f32[1,256,2048]{2,0,1:T(1,128)} %copy.39), calls=%async_computation | async-start | bytes 4194304 | tf_op jit(solution)/shard_map/all_to_all | solution.py:106
  160.5 2.4 copy-start.8
  165.8 3.5 copy-start.4
  172.6 34.3 %all-to-all-start.1 = ((f32[64,4,1024]{2,1,0:T(4,128)}), f32[64,4,1024]{2,1,0:T(4,128)}, u32[]{:S(2)}, u32[]{:S(2)}) async-start(f32[64,4,1024]{2,1,0:T(4,128)} %copy.44), calls=%async_computation.1 | async-start | bytes 2097152 | tf_op jit(solution)/shard_map/all_to_all | solution.py:121
  178.2 2.8 copy-start.12
  206.9 34.7 %all-to-all-start.3 = ((bf16[64,4,2048]{2,1,0:T(4,128)(2,1)}), bf16[64,4,2048]{2,1,0:T(4,128)(2,1)S(1)}, u32[]{:S(2)}, u32[]{:S(2)}) async-start(bf16[64,4,2048]{2,1,0:T(4,128)(2,1)} %copy.48), calls=%async_computation.4 | async-start | bytes 2097152 | tf_op jit(solution)/shard_map/all_to_all | solution.py:161
  212.8 68.2 %reduce-scatter.3.cloned.1.call-start = ((), (), s32[]{:S(2)}) async-start(), calls=%async_computation.6 | async-start | bytes 2621440 | tf_op jit(solution)/shard_map/reduce_scatter | solution.py:132
  217.7 26.8 %copy-start.17 = (f32[128,512]{1,0:T(8,128)S(1)}, f32[128,512]{1,0:T(8,128)}, u32[]{:S(2)}) copy-start(f32[128,512]{1,0:T(8,128)} %copy-done.16) | copy-start | bytes 786436
  217.7 26.8 %copy-start.20 = (f32[512]{0:T(512)S(1)}, f32[512]{0:T(512)}, u32[]{:S(2)}) copy-start(f32[512]{0:T(512)} %param.13) | copy-start | bytes 6148
  218.5 28.0 %copy-start.19 = (f32[128,512]{1,0:T(8,128)S(1)}, f32[128,512]{1,0:T(8,128)}, u32[]{:S(2)}) copy-start(f32[128,512]{1,0:T(8,128)} %get-tuple-element.42) | copy-start | bytes 786436
  218.5 28.0 %collective-permute-start.1 = (f32[128,512]{1,0:T(8,128)S(1)}, f32[128,512]{1,0:T(8,128)}, u32[]{:S(2)}, u32[]{:S(2)}) collective-permute-start(f32[128,512]{1,0:T(8,128)S(1)} %slice.148), channel_id=1, source_target_pairs={{0,4},{4,8},{8,12},{12,16},{16,20},{20,24},{24,28},{28,32},{32,36}... | collective-permute-start | bytes 786440 | tf_op jit(solution)/shard_map/ppermute | solution.py:13
  221.4 25.1 %copy-start.15 = (f32[256,512]{1,0:T(8,128)S(1)}, f32[256,512]{1,0:T(8,128)}, u32[]{:S(2)}) copy-start(f32[256,512]{1,0:T(8,128)} %copy-done.14) | copy-start | bytes 1572868
  242.8 4.8 %copy-start.7 = (f32[3,128,512]{2,1,0:T(8,128)S(1)}, f32[3,128,512]{2,1,0:T(8,128)}, u32[]{:S(2)}) copy-start(f32[3,128,512]{2,1,0:T(8,128)} %copy-done.6) | copy-start | bytes 2359300
  244.5 3.1 copy-start.2
  249.8 189.7 %reduce-scatter.5.cloned.1.call-start = ((), (), s32[]{:S(2)}) async-start(), calls=%async_computation.8 | async-start | bytes 10649600 | tf_op jit(solution)/shard_map/reduce_scatter | solution.py:204
  250.0 15.1 %collective-permute-start.3 = (f32[3,2,512]{2,1,0:T(2,128)S(1)}, f32[3,2,512]{2,1,0:T(2,128)S(1)}, u32[]{:S(2)}, u32[]{:S(2)}) collective-permute-start(f32[3,2,512]{2,1,0:T(2,128)S(1)} %slice.153), channel_id=1, source_target_pairs={{4,0},{8,4},{12,8},{16,12},{20,16},{24,20},{28,24},{32,28},{36,32}... | collective-permute-start | bytes 36872 | tf_op jit(solution)/shard_map/ppermute | solution.py:13
  277.9 165.8 %copy-start.1 = (f32[128,512]{1,0:T(8,128)S(1)}, f32[128,512]{1,0:T(8,128)}, u32[]{:S(2)}) copy-start(f32[128,512]{1,0:T(8,128)} %param.12) | copy-start | bytes 786436
  (8 other events, 12.0 us)
Sparse Core Ops, SparseCore 0:
  9.8 28.5 all-gather.1
  249.9 27.6 reduce-scatter.2
  282.5 156.9 reduce-scatter.4
where the time goes:
time: 460 us; the launch traced here: 451 us
  waiting for transfers between devices  269 us (58%)
  matrix products  54.6 us (12%)
  local copies, waits for them, and re-layouts  46.4 us (10%)
  starting transfers between devices  38.5 us (8%)
  other arithmetic  27.3 us (6%)
  between operations  14.9 us (3%)
    reduce_scatter x1, waiting for transfers between devices, on_device(): lax.psum_scatter(combined.reshape(-1, channel_count), 'seq', scatter_dime...  157 us
    dot_general x36, matrix products, along_rows(): return jnp.tensordot(factor, values, axes=1, precision=exact_mode)  43.2 us
    all_to_all x1, waiting for transfers between devices, on_device(): lax.all_to_all(jnp.concatenate([input_pair[0], input_pair[1], filter_pair...  33.2 us
    all_gather x1, waiting for transfers between devices, on_device(): full_cotangent = lax.all_gather(cotangent, 'ch', axis=1, tiled=True)  25.7 us
    all_to_all x1, waiting for transfers between devices, on_device(): lax.all_to_all(jnp.concatenate(inverse_pair, axis=-1), 'seq', split_axis=...  20.8 us
    all_to_all x1, waiting for transfers between devices, on_device(): lax.all_to_all(as_sent(jnp.concatenate(input_back + filter_back, axis=-1)...  20.3 us
    all_to_all x1, starting transfers between devices, on_device(): lax.all_to_all(jnp.concatenate(grad_pair, axis=1)[None].astype(jnp.bfloat...  13.8 us
    all_to_all x1, waiting for transfers between devices, on_device(): lax.all_to_all(jnp.concatenate(grad_pair, axis=1)[None].astype(jnp.bfloat...  9.73 us
  transfers between devices with their start and end apart: 11, of which 7 were waited for; matrix products, arithmetic and copies ran while one was open for 16% of the time, Pallas kernels for 0%

commit v1 on v0

--- a/solution.py
+++ b/solution.py
@@ -5,6 +5,12 @@
 from jax.sharding import PartitionSpec as P
 
 exact_mode = lax.Precision.HIGHEST
+
+
+def in_order(pieces, dim):
+    shape = list(pieces.shape[1:])
+    shape[dim] *= pieces.shape[0]
+    return jnp.moveaxis(pieces, 0, dim).reshape(shape)
 
 
 def from_behind(shard, axis, by):
@@ -132,7 +138,19 @@
     layer_out = lax.psum_scatter(partial_value, "ch", scatter_dimension=1, tiled=True).astype(
         jnp.bfloat16
     )
-    full_cotangent = lax.all_gather(cotangent, "ch", axis=1, tiled=True)
+    devices = lax.axis_size("ch")
+    pairs_2 = [(i_2, (i_2 + 1) % devices) for i_2 in range(devices)]
+    back = [(b, a) for a, b in pairs_2]
+    lower, upper = ([], [])
+    for step in range(devices - 1):
+        if step % 2 == 0:
+            lower.append(lax.ppermute(lower[-1] if lower else cotangent, "ch", pairs_2))
+        else:
+            upper.append(lax.ppermute(upper[-1] if upper else cotangent, "ch", back))
+    blocks = jnp.stack([*lower[::-1], cotangent, *upper])
+    shift = lax.axis_index("ch") - len(lower)
+    blocks = blocks[(jnp.arange(devices) - shift) % devices]
+    full_cotangent = in_order(blocks, 1)
     grad_gated = lax.dot_general(
         full_cotangent, out_weight, (((1,), (1,)), ((), ())), preferred_element_type=jnp.float32
     )

time: 460 us -> 448 us (0.974)
  waiting for transfers between devices: 269 us -> 260 us
  starting transfers between devices: 38.5 us -> 45.2 us
  local copies, waits for them, and re-layouts: 46.4 us -> 40.6 us
    all_gather x1 -> x0, waiting for transfers between devices: 25.7 us -> none  [on_device(): full_cotangent = lax.all_gather(cotangent, 'ch', axis=1, tiled=True)]
    dot_general x1 -> x0, local copies, waits for them, and re-layouts: 9.14 us -> none  [on_device(): lax.dot_general(full_cotangent, gated_values, (((0,), (0,)), ((), ())), p...]
    ppermute x0 -> x3, waiting for transfers between devices: none -> 8.52 us  [the longest x2 8.51 us: on_device(): lower.append(lax.ppermute(lower[-1] if lower else cotangent, 'ch', pairs_2))]
    reduce_scatter x1, waiting for transfers between devices: 0.01 us -> 5.46 us  [on_device(): lax.psum_scatter(partial_value, 'ch', scatter_dimension=1, tiled=True)]
    unnamed x47 -> x51, local copies, waits for them, and re-layouts: 9.71 us -> 9.81 us
  transfers between devices with their start and end apart: 11 -> 13, of which waited for: 7 -> 9; matrix products, arithmetic and copies ran while one was open for 16% -> 14% of each run, Pallas kernels for 0% -> 0%
where the time goes in v1:
time: 448 us; the launch traced here: 443 us
  waiting for transfers between devices  260 us (58%)
  matrix products  54.6 us (12%)
  starting transfers between devices  45.2 us (10%)
  local copies, waits for them, and re-layouts  40.6 us (9%)
  other arithmetic  27.5 us (6%)
  between operations  15.3 us (3%)
    reduce_scatter x1, waiting for transfers between devices, on_device(): lax.psum_scatter(combined.reshape(-1, channel_count), 'seq', scatter_dime...  160 us
    dot_general x36, matrix products, along_rows(): return jnp.tensordot(factor, values, axes=1, precision=exact_mode)  43.2 us
    all_to_all x1, waiting for transfers between devices, on_device(): lax.all_to_all(jnp.concatenate([input_pair[0], input_pair[1], filter_pair...  33.1 us
    all_to_all x1, waiting for transfers between devices, on_device(): lax.all_to_all(jnp.concatenate(inverse_pair, axis=-1), 'seq', split_axis=...  20.8 us
    all_to_all x1, waiting for transfers between devices, on_device(): lax.all_to_all(as_sent(jnp.concatenate(input_back + filter_back, axis=-1)...  20.2 us
    all_to_all x1, starting transfers between devices, on_device(): lax.all_to_all(jnp.concatenate(grad_pair, axis=1)[None].astype(jnp.bfloat...  16.8 us
    unnamed x51, local copies, waits for them, and re-layouts  9.81 us
    all_to_all x1, waiting for transfers between devices, on_device(): lax.all_to_all(jnp.concatenate(grad_pair, axis=1)[None].astype(jnp.bfloat...  9.71 us
  transfers between devices with their start and end apart: 13, of which 9 were waited for; matrix products, arithmetic and copies ran while one was open for 14% of the time, Pallas kernels for 0%

profile of v1, /device:TPU:2, one launch (start us, length us, event | category | flops | bytes accessed | tf_op | source)
XLA Modules:
  0.0 443.1 jit_solution(5134162311349796524)
XLA Ops:
  17.3 6.8 %collective-permute-done.3 = bf16[128,1024]{1,0:T(8,128)(2,1)S(1)} collective-permute-done((bf16[128,1024]{1,0:T(8,128)(2,1)S(1)}, bf16[128,1024]{1,0:T(8,128)(2,1)S(1)}, u32[]{:S(2)}, u32[]{:S(2)}) %collective-permute-start.3) | collective-permute-done | bytes 262176 | tf_op jit(solution)/shard_map/ppermute | solution.py:147
  27.5 4.8 %multiply_reduce_fusion.3 = (f32[512]{0:T(512)S(1)}, f32[128,512]{1,0:T(8,128)S(1)}, f32[128,512]{1,0:T(8,128)S(1)}, f32[128,512]{1,0:T(8,128)}) fusion(f32[3,128,512]{2,1,0:T(8,128)S(1)} %multiply_add_fusion.3, bf16[128,4096]{0,1:T(8,128)(2,1)S(1)} %bitcast.166, bf16[512,4096]{1,0:T(8,128)(2,1)} %param.14), kind=kOutput, calls=%fused_computation.96 | convolution fusion | flops 537132544 | bytes 6817792 | tf_op jit(solution)/shard_map/dot_general | solution.py:154
  40.3 3.7 reduce.3
  45.1 16.8 %all-to-all-start.2 = ((bf16[64,2,2048]{2,1,0:T(2,128)(2,1)}), bf16[64,2,2048]{2,1,0:T(2,128)(2,1)S(1)}, u32[]{:S(2)}, u32[]{:S(2)}) async-start(bf16[64,2,2048]{2,1,0:T(2,128)(2,1)} %reshape.143), calls=%async_computation.3 | async-start | bytes 1048576 | tf_op jit(solution)/shard_map/all_to_all | solution.py:166
  66.3 3.5 copy.44
  69.8 9.7 %all-to-all-done.2 = bf16[64,2,2048]{2,1,0:T(2,128)(2,1)S(1)} async-done(((bf16[64,2,2048]{2,1,0:T(2,128)(2,1)}), bf16[64,2,2048]{2,1,0:T(2,128)(2,1)S(1)}, u32[]{:S(2)}, u32[]{:S(2)}) %all-to-all-start.2) | async-done | bytes 524320 | tf_op jit(solution)/shard_map/all_to_all | solution.py:166
  80.4 5.8 %all-to-all-start = ((f32[1,256,2048]{2,0,1:T(1,128)}), f32[1,256,2048]{2,0,1:T(1,128)S(1)}, u32[]{:S(2)}, u32[]{:S(2)}) async-start(f32[1,256,2048]{2,0,1:T(1,128)} %copy.44), calls=%async_computation | async-start | bytes 4194304 | tf_op jit(solution)/shard_map/all_to_all | solution.py:112
  86.2 4.9 %reshape.144 = bf16[256,1,1024]{2,1,0:T(2,128)(2,1)} reshape(bf16[64,2,2048]{2,1,0:T(2,128)(2,1)} %copy-done.14) | data formatting | bytes 1048576
  91.1 5.1 %bitcast_reduce_fusion = bf16[256,1024]{1,0:T(8,128)(2,1)} fusion(bf16[256,1,1024]{2,1,0:T(2,128)(2,1)} %reshape.144), kind=kLoop, calls=%fused_computation.355 | loop fusion | bytes 1048576 | tf_op jit(solution)/shard_map/all_to_all | solution.py:166
  96.1 2.0 all_to_all.41
  104.4 33.1 %all-to-all-done = f32[1,256,2048]{2,0,1:T(1,128)S(1)} async-done(((f32[1,256,2048]{2,0,1:T(1,128)}), f32[1,256,2048]{2,0,1:T(1,128)S(1)}, u32[]{:S(2)}, u32[]{:S(2)}) %all-to-all-start) | async-done | bytes 2097184 | tf_op jit(solution)/shard_map/all_to_all | solution.py:112
  137.5 6.8 %reduce = f32[256,2048]{1,0:T(8,128)} reduce(f32[1,256,2048]{2,0,1:T(1,128)S(1)} %all-to-all-done, f32[]{:T(128)} %constant.94), dimensions={0}, to_apply=%all_to_all.16.reduce_sub_computation | reduce | bytes 4194308 | tf_op jit(solution)/shard_map/all_to_all | solution.py:112
  144.3 2.0 all_to_all.17
  155.1 2.8 multiply_add_fusion.1
  164.7 5.6 %all-to-all-start.1 = ((f32[64,4,1024]{2,1,0:T(4,128)}), f32[64,4,1024]{2,1,0:T(4,128)}, u32[]{:S(2)}, u32[]{:S(2)}) async-start(f32[64,4,1024]{2,1,0:T(4,128)} %copy.49), calls=%async_computation.1 | async-start | bytes 2097152 | tf_op jit(solution)/shard_map/all_to_all | solution.py:127
  178.3 20.8 %all-to-all-done.1 = f32[64,4,1024]{2,1,0:T(4,128)} async-done(((f32[64,4,1024]{2,1,0:T(4,128)}), f32[64,4,1024]{2,1,0:T(4,128)}, u32[]{:S(2)}, u32[]{:S(2)}) %all-to-all-start.1) | async-done | bytes 1048608 | tf_op jit(solution)/shard_map/all_to_all | solution.py:127
  199.0 5.8 %all-to-all-start.3 = ((bf16[64,4,2048]{2,1,0:T(4,128)(2,1)}), bf16[64,4,2048]{2,1,0:T(4,128)(2,1)S(1)}, u32[]{:S(2)}, u32[]{:S(2)}) async-start(bf16[64,4,2048]{2,1,0:T(4,128)(2,1)} %copy.54), calls=%async_computation.4 | async-start | bytes 2097152 | tf_op jit(solution)/shard_map/all_to_all | solution.py:179
  210.6 2.9 collective-permute-start.1
  213.5 20.2 %all-to-all-done.3 = bf16[64,4,2048]{2,1,0:T(4,128)(2,1)S(1)} async-done(((bf16[64,4,2048]{2,1,0:T(4,128)(2,1)}), bf16[64,4,2048]{2,1,0:T(4,128)(2,1)S(1)}, u32[]{:S(2)}, u32[]{:S(2)}) %all-to-all-start.3) | async-done | bytes 1048608 | tf_op jit(solution)/shard_map/all_to_all | solution.py:179
  239.8 2.1 fusion.307
  243.5 4.5 %fusion.55 = f32[64,64,512]{2,1,0:T(8,128)} fusion(bf16[64,64,128]{2,1,0:T(8,128)(2,1)S(1)} %bitcast.167, bf16[128,512]{1,0:T(8,128)(2,1)S(1)} %get-tuple-element.36), kind=kOutput, calls=%fused_computation.124 | convolution fusion | flops 536870912 | bytes 9568256 | tf_op jit(solution)/shard_map/dot_general | solution.py:157
  249.9 9.6 %pad_maximum_fusion = f32[64,80,512]{2,1,0:T(8,128)} fusion(f32[64,16,512]{2,1,0:T(8,128)S(1)} %broadcast_in_dim.19, f32[64,64,512]{2,1,0:T(8,128)} %fusion.55), kind=kLoop, calls=%fused_computation.1 | loop fusion | flops 2621440 | bytes 20971520 | tf_op jit(solution)/shard_map/concatenate | solution.py:218
  263.9 5.5 %reduce-scatter.3.cloned.1.call-done = f32[128,1024]{1,0:T(8,128)} async-done(((f32[128,4096]{1,0:T(8,128)}), f32[128,1024]{1,0:T(8,128)}) %reduce-scatter.3.cloned.1.call-update) | async-done | bytes 524304 | tf_op jit(solution)/shard_map/reduce_scatter | solution.py:138
  271.1 160.4 %reduce-scatter.5.cloned.1.call-done = f32[80,512]{1,0:T(8,128)} async-done(((f32[5120,512]{1,0:T(8,128)}), f32[80,512]{1,0:T(8,128)}) %reduce-scatter.5.cloned.1.call-update) | async-done | bytes 163856 | tf_op jit(solution)/shard_map/reduce_scatter | solution.py:222
  (145 shorter events, 82.5 us)
Async XLA Ops:
  7.2 54.7 %copy-start = (f32[128,512]{1,0:T(8,128)S(1)}, f32[128,512]{1,0:T(8,128)}, u32[]{:S(2)}) copy-start(f32[128,512]{1,0:T(8,128)} %param.12) | copy-start | bytes 786436
  7.2 8.3 %collective-permute-start.2 = (bf16[128,1024]{1,0:T(8,128)(2,1)}, bf16[128,1024]{1,0:T(8,128)(2,1)S(1)}, u32[]{:S(2)}, u32[]{:S(2)}) collective-permute-start(bf16[128,1024]{1,0:T(8,128)(2,1)} %param.15), channel_id=1, source_target_pairs={{0,1},{1,2},{2,3},{3,0},{4,5},{5,6},{6,7},{7,4},{8,9},{9,10},{10,1... | collective-permute-start | bytes 786440 | tf_op jit(solution)/shard_map/ppermute | solution.py:147
  8.8 8.5 %collective-permute-start.4 = (bf16[128,1024]{1,0:T(8,128)(2,1)}, bf16[128,1024]{1,0:T(8,128)(2,1)S(1)}, u32[]{:S(2)}, u32[]{:S(2)}) collective-permute-start(bf16[128,1024]{1,0:T(8,128)(2,1)} %param.15), channel_id=1, source_target_pairs={{1,0},{2,1},{3,2},{0,3},{5,4},{6,5},{7,6},{4,7},{9,8},{10,9},{11,1... | collective-permute-start | bytes 786440 | tf_op jit(solution)/shard_map/ppermute | solution.py:149
  10.4 2.2 collective-permute-start
  12.6 11.5 %copy-start.21 = (bf16[128,1024]{1,0:T(8,128)(2,1)S(1)}, bf16[128,1024]{1,0:T(8,128)(2,1)}, u32[]{:S(2)}) copy-start(bf16[128,1024]{1,0:T(8,128)(2,1)} %param.15) | copy-start | bytes 786436
  15.5 8.6 %collective-permute-start.3 = (bf16[128,1024]{1,0:T(8,128)(2,1)S(1)}, bf16[128,1024]{1,0:T(8,128)(2,1)S(1)}, u32[]{:S(2)}, u32[]{:S(2)}) collective-permute-start(bf16[128,1024]{1,0:T(8,128)(2,1)S(1)} %collective-permute-done.2), channel_id=1, source_target_pairs={{0,1},{1,2},{2,3},{3,0},{4,5},{5,6},{6,7},{7,4},{8,9},{9,10},{10,1... | collective-permute-start | bytes 786440 | tf_op jit(solution)/shard_map/ppermute | solution.py:147
  17.3 10.2 %copy-start.8 = (f32[3,128,512]{2,1,0:T(8,128)}, f32[3,128,512]{2,1,0:T(8,128)S(1)}, u32[]{:S(2)}) copy-start(f32[3,128,512]{2,1,0:T(8,128)S(1)} %multiply_add_fusion.3) | copy-start | bytes 2359300
  27.5 4.8 %copy-start.6 = (bf16[128,4,1024]{0,2,1:T(8,128)(2,1)}, bf16[128,4,1024]{0,2,1:T(8,128)(2,1)S(1)}, u32[]{:S(2)}) copy-start(bf16[128,4,1024]{0,2,1:T(8,128)(2,1)S(1)} %copy.50) | copy-start | bytes 3145732
  32.3 6.6 %copy-start.17 = (f32[128,512]{1,0:T(8,128)}, f32[128,512]{1,0:T(8,128)S(1)}, u32[]{:S(2)}) copy-start(f32[128,512]{1,0:T(8,128)S(1)} %get-tuple-element.12) | copy-start | bytes 786436
  32.3 3.2 collective-permute-start.5
  45.1 34.5 %all-to-all-start.2 = ((bf16[64,2,2048]{2,1,0:T(2,128)(2,1)}), bf16[64,2,2048]{2,1,0:T(2,128)(2,1)S(1)}, u32[]{:S(2)}, u32[]{:S(2)}) async-start(bf16[64,2,2048]{2,1,0:T(2,128)(2,1)} %reshape.143), calls=%async_computation.3 | async-start | bytes 1048576 | tf_op jit(solution)/shard_map/all_to_all | solution.py:166
  80.4 57.2 %all-to-all-start = ((f32[1,256,2048]{2,0,1:T(1,128)}), f32[1,256,2048]{2,0,1:T(1,128)S(1)}, u32[]{:S(2)}, u32[]{:S(2)}) async-start(f32[1,256,2048]{2,0,1:T(1,128)} %copy.44), calls=%async_computation | async-start | bytes 4194304 | tf_op jit(solution)/shard_map/all_to_all | solution.py:112
  164.7 34.4 %all-to-all-start.1 = ((f32[64,4,1024]{2,1,0:T(4,128)}), f32[64,4,1024]{2,1,0:T(4,128)}, u32[]{:S(2)}, u32[]{:S(2)}) async-start(f32[64,4,1024]{2,1,0:T(4,128)} %copy.49), calls=%async_computation.1 | async-start | bytes 2097152 | tf_op jit(solution)/shard_map/all_to_all | solution.py:127
  199.0 34.7 %all-to-all-start.3 = ((bf16[64,4,2048]{2,1,0:T(4,128)(2,1)}), bf16[64,4,2048]{2,1,0:T(4,128)(2,1)S(1)}, u32[]{:S(2)}, u32[]{:S(2)}) async-start(bf16[64,4,2048]{2,1,0:T(4,128)(2,1)} %copy.54), calls=%async_computation.4 | async-start | bytes 2097152 | tf_op jit(solution)/shard_map/all_to_all | solution.py:179
  204.8 64.5 %reduce-scatter.3.cloned.1.call-start = ((), (), s32[]{:S(2)}) async-start(), calls=%async_computation.6 | async-start | bytes 2621440 | tf_op jit(solution)/shard_map/reduce_scatter | solution.py:138
  209.8 26.9 %copy-start.18 = (f32[128,512]{1,0:T(8,128)S(1)}, f32[128,512]{1,0:T(8,128)}, u32[]{:S(2)}) copy-start(f32[128,512]{1,0:T(8,128)} %copy-done.17) | copy-start | bytes 786436
  209.8 26.9 %copy-start.22 = (f32[512]{0:T(512)S(1)}, f32[512]{0:T(512)}, u32[]{:S(2)}) copy-start(f32[512]{0:T(512)} %param.13) | copy-start | bytes 6148
  210.6 28.0 %copy-start.20 = (f32[128,512]{1,0:T(8,128)S(1)}, f32[128,512]{1,0:T(8,128)}, u32[]{:S(2)}) copy-start(f32[128,512]{1,0:T(8,128)} %get-tuple-element.42) | copy-start | bytes 786436
  210.6 28.0 %collective-permute-start.1 = (f32[128,512]{1,0:T(8,128)S(1)}, f32[128,512]{1,0:T(8,128)}, u32[]{:S(2)}, u32[]{:S(2)}) collective-permute-start(f32[128,512]{1,0:T(8,128)S(1)} %slice.150), channel_id=1, source_target_pairs={{0,4},{4,8},{8,12},{12,16},{16,20},{20,24},{24,28},{28,32},{32,36}... | collective-permute-start | bytes 786440 | tf_op jit(solution)/shard_map/ppermute | solution.py:19
  213.5 25.1 %copy-start.16 = (f32[256,512]{1,0:T(8,128)S(1)}, f32[256,512]{1,0:T(8,128)}, u32[]{:S(2)}) copy-start(f32[256,512]{1,0:T(8,128)} %copy-done.15) | copy-start | bytes 1572868
  234.8 4.8 %copy-start.9 = (f32[3,128,512]{2,1,0:T(8,128)S(1)}, f32[3,128,512]{2,1,0:T(8,128)}, u32[]{:S(2)}) copy-start(f32[3,128,512]{2,1,0:T(8,128)} %copy-done.8) | copy-start | bytes 2359300
  241.9 189.7 %reduce-scatter.5.cloned.1.call-start = ((), (), s32[]{:S(2)}) async-start(), calls=%async_computation.7 | async-start | bytes 10649600 | tf_op jit(solution)/shard_map/reduce_scatter | solution.py:222
  242.1 6.0 %collective-permute-start.6 = (f32[3,2,512]{2,1,0:T(2,128)S(1)}, f32[3,2,512]{2,1,0:T(2,128)S(1)}, u32[]{:S(2)}, u32[]{:S(2)}) collective-permute-start(f32[3,2,512]{2,1,0:T(2,128)S(1)} %slice.155), channel_id=1, source_target_pairs={{4,0},{8,4},{12,8},{16,12},{20,16},{24,20},{28,24},{32,28},{36,32}... | collective-permute-start | bytes 36872 | tf_op jit(solution)/shard_map/ppermute | solution.py:19
  260.8 175.0 %copy-start.1 = (f32[128,512]{1,0:T(8,128)S(1)}, f32[128,512]{1,0:T(8,128)}, u32[]{:S(2)}) copy-start(f32[128,512]{1,0:T(8,128)} %param.12) | copy-start | bytes 786436
  (12 other events, 23.8 us)
Sparse Core Ops, SparseCore 0:
  242.0 27.3 reduce-scatter.2
  274.2 157.2 reduce-scatter.4
